TPU v7x, 256 devices: a whole 4x4x8 slice. The times are simulated.
256 devices in a mesh: seq: 32 (over x, z), ch: 8 (over y, core).
Axes of the slice: x: 4, y: 4, z: 8, core: 2. Of those that a mesh axis runs over, the one named last changes fastest.
Arguments:
- out_gate: bfloat16 [12288, 4096], P('seq', 'ch'), may hold values from -6 to 6
- in_gate: bfloat16 [12288, 4096], P('seq', 'ch'), may hold values from -6 to 6
- values: bfloat16 [12288, 4096], P('seq', 'ch'), may hold values from -6 to 6
- short_filter: float32 [3, 3, 4096], P(None, None, 'ch'), may hold values from -3 to 3
- long_filter: float32 [12288, 4096], P('seq', 'ch'), may hold values from -1.5 to 1.5
- skip_gain: float32 [4096], P('ch'), may hold values from -4 to 4
- out_weight: bfloat16 [4096, 4096], P(None, 'ch'), may hold values from -0.09375 to 0.09375
Outputs:
- projected: bfloat16 [12288, 4096], P('seq', 'ch')
All inputs are finite; a program needn't handle non-finite values.
Results may differ from a plain program's by a relative error of at most 0.0049.
Values may be sent and summed in bfloat16 or wider, within the bound.
A program may use at most 128 MiB of HBM per device.

v0:
```python
import math
import jax
import jax.numpy as jnp
from jax import lax
from jax.sharding import PartitionSpec as P

highest = lax.Precision.HIGHEST


def shifted(block, axis, distance):
    devices = range(lax.axis_size(axis))
    route = [(i - distance, i) for i in devices if i - distance in devices]
    return lax.ppermute(block, axis, route)


def phase_table(row_ids, col_ids, modulus, direction):
    product = row_ids[:, None] * col_ids[None, :] % modulus
    angles = product.astype(jnp.float32) * (direction * 2.0 * math.pi / modulus)
    return (jnp.cos(angles), jnp.sin(angles))


def contract(pattern, first_op, second_op):
    return jnp.einsum(pattern, first_op, second_op, precision=highest)


def complex_apply(pattern, phases, operand):
    cosine, sine_part = phases
    real_part, imaginary = operand
    return (
        contract(pattern, cosine, real_part) - contract(pattern, sine_part, imaginary),
        contract(pattern, cosine, imaginary) + contract(pattern, sine_part, real_part),
    )


def complex_times(first_op, second_op):
    return (
        first_op[0] * second_op[0] - first_op[1] * second_op[1],
        first_op[0] * second_op[1] + first_op[1] * second_op[0],
    )


def sequence_conv(mixed_in, long_filter):
    seq_count = lax.axis_size("seq")
    seq_index = lax.axis_index("seq")
    row_count = mixed_in.shape[0]
    total_len = row_count * seq_count
    piece_rows = row_count // seq_count
    rows_b = jnp.arange(row_count, dtype=jnp.int32)
    device_ids = jnp.arange(seq_count, dtype=jnp.int32)
    positions = seq_index * row_count + rows_b
    angles = positions.astype(jnp.float32) * (math.pi / total_len)
    cosines = jnp.cos(angles)[:, None]
    sines = jnp.sin(angles)[:, None]
    planes = jnp.stack([mixed_in, long_filter])[:, None]
    spread = lax.all_to_all(planes, "seq", split_axis=2, concat_axis=1, tiled=True)
    local_b = seq_index * piece_rows + jnp.arange(piece_rows, dtype=jnp.int32)
    arrived_pos = device_ids[:, None] * row_count + local_b[None, :]
    arrived_angles = arrived_pos.astype(jnp.float32) * (math.pi / total_len)
    arrived_cos = jnp.cos(arrived_angles)[:, :, None]
    arrived_sin = jnp.sin(arrived_angles)[:, :, None]
    zeros_plane = jnp.zeros_like(spread[0])
    real_part = jnp.stack([spread[0], spread[0] * arrived_cos, spread[1], spread[1] * arrived_cos])
    imaginary = jnp.stack(
        [zeros_plane, -spread[0] * arrived_sin, zeros_plane, -spread[1] * arrived_sin]
    )
    sectioned = complex_apply(
        "kp,xpbc->xkbc",
        phase_table(device_ids, device_ids, seq_count, -1.0),
        (real_part, imaginary),
    )
    twist_table = phase_table(device_ids, local_b, total_len, -1.0)
    sectioned = complex_times(sectioned, (twist_table[0][:, :, None], twist_table[1][:, :, None]))
    arrived = (
        lax.all_to_all(sectioned[0], "seq", split_axis=1, concat_axis=2, tiled=True),
        lax.all_to_all(sectioned[1], "seq", split_axis=1, concat_axis=2, tiled=True),
    )
    spectra = complex_apply("mb,xkbc->xkmc", phase_table(rows_b, rows_b, row_count, -1.0), arrived)
    product = complex_times((spectra[0][:2], spectra[1][:2]), (spectra[0][2:], spectra[1][2:]))
    sectioned = complex_apply("mb,xkmc->xkbc", phase_table(rows_b, rows_b, row_count, 1.0), product)
    twist_table = phase_table(seq_index.reshape(1), rows_b, total_len, 1.0)
    sectioned = complex_times(sectioned, (twist_table[0][:, :, None], twist_table[1][:, :, None]))
    returned = (
        lax.all_to_all(sectioned[0], "seq", split_axis=2, concat_axis=1, tiled=True),
        lax.all_to_all(sectioned[1], "seq", split_axis=2, concat_axis=1, tiled=True),
    )
    sectioned = complex_apply(
        "kp,xkbc->xpbc", phase_table(device_ids, device_ids, seq_count, 1.0), returned
    )
    restored = (
        lax.all_to_all(sectioned[0], "seq", split_axis=1, concat_axis=2, tiled=True),
        lax.all_to_all(sectioned[1], "seq", split_axis=1, concat_axis=2, tiled=True),
    )
    real_out = restored[0][:, 0] / total_len
    imag_out = restored[1][:, 0] / total_len
    return 0.5 * (real_out[0] + cosines * real_out[1] - sines * imag_out[1])


def on_device(out_gate, in_gate, values, short_filter, long_filter, skip_gain, out_weight):
    tap_count = short_filter.shape[1]
    row_count = out_gate.shape[0]
    stacked = jnp.stack([out_gate, in_gate, values])
    rim_rows = shifted(stacked[:, row_count - (tap_count - 1) :], "seq", 1)
    widened = jnp.concatenate([rim_rows, stacked], axis=1).astype(jnp.float32)
    shorted = short_filter[:, 0, None, :] * widened[:, tap_count - 1 :]
    for offset in range(1, tap_count):
        start_row = tap_count - 1 - offset
        shorted = (
            shorted
            + short_filter[:, offset, None, :] * widened[:, start_row : start_row + row_count]
        )
    gate_late = shorted[0]
    mixed_in = shorted[1] * shorted[2]
    long_out = sequence_conv(mixed_in, long_filter)
    filtered = long_out + skip_gain * mixed_in
    mixed = (gate_late * filtered).astype(jnp.bfloat16)
    summed = jnp.dot(
        lax.all_gather(mixed, "ch", axis=1, tiled=True),
        out_weight,
        preferred_element_type=jnp.float32,
    )
    return summed.astype(jnp.bfloat16)


def solution(mesh):
    return jax.shard_map(
        on_device,
        mesh=mesh,
        in_specs=(
            P("seq", "ch"),
            P("seq", "ch"),
            P("seq", "ch"),
            P(None, None, "ch"),
            P("seq", "ch"),
            P("ch"),
            P(None, "ch"),
        ),
        out_specs=P("seq", "ch"),
        check_vma=False,
    )
```

profile of v0, /device:TPU:1, one launch (start us, length us, event | category | flops | bytes accessed | tf_op | source)
XLA Modules:
  0.0 544.4 jit_solution(16303291833496536461)
XLA Ops:
  19.1 12.4 %all-to-all-start = ((f32[2,1,384,512]{3,0,1,2:T(2,128)}), f32[2,1,384,512]{3,0,1,2:T(2,128)S(1)}, u32[]{:S(2)}, u32[]{:S(2)}) async-start(f32[2,1,384,512]{3,0,1,2:T(2,128)} %copy.68), calls=%async_computation | async-start | bytes 3145728 | tf_op jit(solution)/shard_map/all_to_all | solution.py:55
  31.7 36.7 %all-to-all-done = f32[2,1,384,512]{3,0,1,2:T(2,128)S(1)} async-done(((f32[2,1,384,512]{3,0,1,2:T(2,128)}), f32[2,1,384,512]{3,0,1,2:T(2,128)S(1)}, u32[]{:S(2)}, u32[]{:S(2)}) %all-to-all-start) | async-done | bytes 1572896 | tf_op jit(solution)/shard_map/all_to_all | solution.py:55
  80.6 6.0 %fusion = (f32[4,32,12,512]{3,1,2,0:T(8,128)S(1)}, f32[4,32,12,512]{3,1,2,0:T(8,128)}) fusion(f32[4,12,512,32]{2,3,1,0:T(8,128)S(1)} %convolution_subtract_fusion, f32[32,12]{0,1:T(8,128)S(1)} %get-tuple-element.27, f32[32,12]{0,1:T(8,128)S(1)} %get-tuple-element.26, f32[4,12,512,32]{2,3,1,0:T(8,128)S(1)} %fusion.2, ...), kind=kOutput, calls=%fused_computation.4 | convolution fusion | flops 309868544 | bytes 15731712 | tf_op jit(solution)/shard_map/kp,xpbc->xkbc/dot_general | solution.py:23
  90.3 7.3 %all-to-all-start.1 = ((f32[4,32,12,512]{3,0,2,1:T(4,128)}), f32[4,32,12,512]{3,0,2,1:T(4,128)S(1)}, u32[]{:S(2)}, u32[]{:S(2)}) async-start(f32[4,32,12,512]{3,0,2,1:T(4,128)} %copy.79), calls=%async_computation.1 | async-start | bytes 6291456 | tf_op jit(solution)/shard_map/all_to_all | solution.py:74
  97.6 5.5 %copy.81 = f32[4,32,12,512]{3,0,2,1:T(4,128)} copy(f32[4,32,12,512]{3,1,2,0:T(8,128)} %get-tuple-element.8) | data formatting | bytes 6291456 | tf_op jit(solution)/shard_map/add | solution.py:38
  103.1 65.8 %all-to-all-done.1 = f32[4,32,12,512]{3,0,2,1:T(4,128)S(1)} async-done(((f32[4,32,12,512]{3,0,2,1:T(4,128)}), f32[4,32,12,512]{3,0,2,1:T(4,128)S(1)}, u32[]{:S(2)}, u32[]{:S(2)}) %all-to-all-start.1) | async-done | bytes 3145760 | tf_op jit(solution)/shard_map/all_to_all | solution.py:74
  170.6 7.8 %all-to-all-start.2 = ((f32[4,32,12,512]{3,0,2,1:T(4,128)}), f32[4,32,12,512]{3,0,2,1:T(4,128)}, u32[]{:S(2)}, u32[]{:S(2)}) async-start(f32[4,32,12,512]{3,0,2,1:T(4,128)} %copy.81), calls=%async_computation.2 | async-start | bytes 6291456 | tf_op jit(solution)/shard_map/all_to_all | solution.py:75
  181.7 9.8 %fusion.43 = f32[4,512,384]{2,1,0:T(8,128)} fusion(f32[4,384,512]{1,2,0:T(8,128)S(1)} %copy.80), kind=kOutput, calls=%fused_computation.73 | convolution fusion | flops 3625205760 | bytes 6291456 | tf_op jit(solution)/shard_map/mb,xkbc->xkmc/dot_general | solution.py:23
  191.5 60.2 %all-to-all-done.2 = f32[4,32,12,512]{3,0,2,1:T(4,128)} async-done(((f32[4,32,12,512]{3,0,2,1:T(4,128)}), f32[4,32,12,512]{3,0,2,1:T(4,128)}, u32[]{:S(2)}, u32[]{:S(2)}) %all-to-all-start.2) | async-done | bytes 3145760 | tf_op jit(solution)/shard_map/all_to_all | solution.py:75
  256.8 10.7 %fusion.41 = f32[4,512,384]{2,1,0:T(8,128)S(1)} fusion(f32[4,384,512]{1,2,0:T(8,128)} %copy.82), kind=kOutput, calls=%fused_computation.71 | convolution fusion | flops 3625205760 | bytes 6291456 | tf_op jit(solution)/shard_map/mb,xkbc->xkmc/dot_general | solution.py:23
  267.6 9.2 %subtract_bitcast_fusion = f32[4,1,384,512]{2,3,0,1:T(8,128)S(1)} fusion(f32[4,512,384]{2,1,0:T(8,128)S(1)} %copy-done.4, f32[4,384,512]{1,2,0:T(8,128)S(1)} %copy-done), kind=kOutput, calls=%fused_computation.9 | convolution fusion | flops 3625992192 | bytes 9437184 | tf_op jit(solution)/shard_map/mb,xkbc->xkmc/dot_general | solution.py:23
  276.8 9.0 %add_bitcast_fusion = f32[4,1,384,512]{2,3,0,1:T(8,128)S(1)} fusion(f32[4,512,384]{2,1,0:T(8,128)S(1)} %fusion.41, f32[4,384,512]{1,2,0:T(8,128)S(1)} %copy.80), kind=kOutput, calls=%fused_computation.8 | convolution fusion | flops 3625992192 | bytes 9437184 | tf_op jit(solution)/shard_map/mb,xkbc->xkmc/dot_general | solution.py:23
  291.5 5.8 %fusion.10 = f32[2,512,384]{2,1,0:T(8,128)S(1)} fusion(f32[2,1,384,512]{2,3,0,1:T(8,128)S(1)} %get-tuple-element.10), kind=kOutput, calls=%fused_computation.28 | convolution fusion | flops 1813266432 | bytes 3145728 | tf_op jit(solution)/shard_map/mb,xkmc->xkbc/dot_general | solution.py:23
  302.8 5.5 %fusion.7 = (f32[2,1,384,512]{2,3,0,1:T(8,128)S(1)}, f32[2,1,384,512]{2,3,0,1:T(8,128)S(1)}) fusion(f32[2,512,384]{2,1,0:T(8,128)S(1)} %fusion.18, f32[384]{0:T(512)S(1)} %get-tuple-element.32, f32[384]{0:T(512)S(1)} %get-tuple-element.33, f32[2,512,384]{2,1,0:T(8,128)S(1)} %fusion.10, f32[2,1,384,512]{2,3,0,1:T(8,128)S(1)} %get-tuple-element.9), kind=kOutput, calls=%fused_computation.23 | convolution fusion | flops 1816018944 | bytes 7867392 | tf_op jit(solution)/shard_map/mb,xkmc->xkbc/dot_general | solution.py:23
  310.4 5.9 %all-to-all-start.3 = ((f32[2,1,384,512]{3,0,1,2:T(2,128)}), f32[2,1,384,512]{3,0,1,2:T(2,128)S(1)}, u32[]{:S(2)}, u32[]{:S(2)}) async-start(f32[2,1,384,512]{3,0,1,2:T(2,128)} %copy.85), calls=%async_computation.3 | async-start | bytes 3145728 | tf_op jit(solution)/shard_map/all_to_all | solution.py:83
  318.3 34.6 %all-to-all-done.3 = f32[2,1,384,512]{3,0,1,2:T(2,128)S(1)} async-done(((f32[2,1,384,512]{3,0,1,2:T(2,128)}), f32[2,1,384,512]{3,0,1,2:T(2,128)S(1)}, u32[]{:S(2)}, u32[]{:S(2)}) %all-to-all-start.3) | async-done | bytes 1572896 | tf_op jit(solution)/shard_map/all_to_all | solution.py:83
  352.9 7.7 %all-to-all-start.4 = ((f32[2,1,384,512]{3,0,1,2:T(2,128)}), f32[2,1,384,512]{3,0,1,2:T(2,128)S(1)}, u32[]{:S(2)}, u32[]{:S(2)}) async-start(f32[2,1,384,512]{3,0,1,2:T(2,128)} %copy.87), calls=%async_computation.4 | async-start | bytes 3145728 | tf_op jit(solution)/shard_map/all_to_all | solution.py:84
  364.3 33.1 %all-to-all-done.4 = f32[2,1,384,512]{3,0,1,2:T(2,128)S(1)} async-done(((f32[2,1,384,512]{3,0,1,2:T(2,128)}), f32[2,1,384,512]{3,0,1,2:T(2,128)S(1)}, u32[]{:S(2)}, u32[]{:S(2)}) %all-to-all-start.4) | async-done | bytes 1572896 | tf_op jit(solution)/shard_map/all_to_all | solution.py:84
  403.9 7.8 %all-to-all-start.5 = ((f32[2,32,12,512]{3,0,2,1:T(2,128)}), f32[2,32,12,512]{3,0,2,1:T(2,128)}, u32[]{:S(2)}, u32[]{:S(2)}) async-start(f32[2,32,12,512]{3,0,2,1:T(2,128)} %copy.89), calls=%async_computation.5 | async-start | bytes 3145728 | tf_op jit(solution)/shard_map/all_to_all | solution.py:90
  419.2 29.2 %all-to-all-done.5 = f32[2,32,12,512]{3,0,2,1:T(2,128)} async-done(((f32[2,32,12,512]{3,0,2,1:T(2,128)}), f32[2,32,12,512]{3,0,2,1:T(2,128)}, u32[]{:S(2)}, u32[]{:S(2)}) %all-to-all-start.5) | async-done | bytes 1572896 | tf_op jit(solution)/shard_map/all_to_all | solution.py:90
  448.4 7.8 %all-to-all-start.6 = ((f32[2,32,12,512]{3,0,2,1:T(2,128)}), f32[2,32,12,512]{3,0,2,1:T(2,128)}, u32[]{:S(2)}, u32[]{:S(2)}) async-start(f32[2,32,12,512]{3,0,2,1:T(2,128)} %copy.92), calls=%async_computation.6 | async-start | bytes 3145728 | tf_op jit(solution)/shard_map/all_to_all | solution.py:91
  464.9 28.1 %all-to-all-done.6 = f32[2,32,12,512]{3,0,2,1:T(2,128)} async-done(((f32[2,32,12,512]{3,0,2,1:T(2,128)}), f32[2,32,12,512]{3,0,2,1:T(2,128)}, u32[]{:S(2)}, u32[]{:S(2)}) %all-to-all-start.6) | async-done | bytes 1572896 | tf_op jit(solution)/shard_map/all_to_all | solution.py:91
  500.7 31.0 %all-gather.2.cloned.1.call-done = bf16[384,4096]{1,0:T(8,128)(2,1)} async-done(((bf16[384,512]{1,0:T(8,128)(2,1)}), bf16[384,4096]{1,0:T(8,128)(2,1)}) %all-gather.2.cloned.1.call-update) | async-done | bytes 3145744 | tf_op jit(solution)/shard_map/all_gather | solution.py:117
  531.6 5.7 %convolution_convert_fusion = bf16[384,512]{1,0:T(8,128)(2,1)} fusion(bf16[384,4096]{1,0:T(8,128)(2,1)} %all-gather.2.cloned.1.call-done, bf16[4096,512]{1,0:T(8,128)(2,1)} %param.13), kind=kOutput, calls=%fused_computation.48 | convolution fusion | flops 1610809344 | bytes 7733248 | tf_op jit(solution)/shard_map/dot_general | solution.py:116
  (60 shorter events, 87.9 us)
Async XLA Ops:
  7.3 5.3 collective-permute-start
  14.9 1.8 copy-start.1
  14.9 1.7 copy-start.5
  19.1 49.3 %all-to-all-start = ((f32[2,1,384,512]{3,0,1,2:T(2,128)}), f32[2,1,384,512]{3,0,1,2:T(2,128)S(1)}, u32[]{:S(2)}, u32[]{:S(2)}) async-start(f32[2,1,384,512]{3,0,1,2:T(2,128)} %copy.68), calls=%async_computation | async-start | bytes 3145728 | tf_op jit(solution)/shard_map/all_to_all | solution.py:55
  90.3 78.6 %all-to-all-start.1 = ((f32[4,32,12,512]{3,0,2,1:T(4,128)}), f32[4,32,12,512]{3,0,2,1:T(4,128)S(1)}, u32[]{:S(2)}, u32[]{:S(2)}) async-start(f32[4,32,12,512]{3,0,2,1:T(4,128)} %copy.79), calls=%async_computation.1 | async-start | bytes 6291456 | tf_op jit(solution)/shard_map/all_to_all | solution.py:74
  168.9 1.7 copy-start.3
  170.6 81.0 %all-to-all-start.2 = ((f32[4,32,12,512]{3,0,2,1:T(4,128)}), f32[4,32,12,512]{3,0,2,1:T(4,128)}, u32[]{:S(2)}, u32[]{:S(2)}) async-start(f32[4,32,12,512]{3,0,2,1:T(4,128)} %copy.81), calls=%async_computation.2 | async-start | bytes 6291456 | tf_op jit(solution)/shard_map/all_to_all | solution.py:75
  256.8 10.7 %copy-start = (f32[4,384,512]{1,2,0:T(8,128)S(1)}, f32[4,384,512]{1,2,0:T(8,128)}, u32[]{:S(2)}) copy-start(f32[4,384,512]{1,2,0:T(8,128)} %copy.82) | copy-start | bytes 9437188
  256.8 10.7 %copy-start.4 = (f32[4,512,384]{2,1,0:T(8,128)S(1)}, f32[4,512,384]{2,1,0:T(8,128)}, u32[]{:S(2)}) copy-start(f32[4,512,384]{2,1,0:T(8,128)} %fusion.43) | copy-start | bytes 9437188
  310.4 42.6 %all-to-all-start.3 = ((f32[2,1,384,512]{3,0,1,2:T(2,128)}), f32[2,1,384,512]{3,0,1,2:T(2,128)S(1)}, u32[]{:S(2)}, u32[]{:S(2)}) async-start(f32[2,1,384,512]{3,0,1,2:T(2,128)} %copy.85), calls=%async_computation.3 | async-start | bytes 3145728 | tf_op jit(solution)/shard_map/all_to_all | solution.py:83
  352.9 44.5 %all-to-all-start.4 = ((f32[2,1,384,512]{3,0,1,2:T(2,128)}), f32[2,1,384,512]{3,0,1,2:T(2,128)S(1)}, u32[]{:S(2)}, u32[]{:S(2)}) async-start(f32[2,1,384,512]{3,0,1,2:T(2,128)} %copy.87), calls=%async_computation.4 | async-start | bytes 3145728 | tf_op jit(solution)/shard_map/all_to_all | solution.py:84
  403.9 44.6 %all-to-all-start.5 = ((f32[2,32,12,512]{3,0,2,1:T(2,128)}), f32[2,32,12,512]{3,0,2,1:T(2,128)}, u32[]{:S(2)}, u32[]{:S(2)}) async-start(f32[2,32,12,512]{3,0,2,1:T(2,128)} %copy.89), calls=%async_computation.5 | async-start | bytes 3145728 | tf_op jit(solution)/shard_map/all_to_all | solution.py:90
  448.4 44.6 %all-to-all-start.6 = ((f32[2,32,12,512]{3,0,2,1:T(2,128)}), f32[2,32,12,512]{3,0,2,1:T(2,128)}, u32[]{:S(2)}, u32[]{:S(2)}) async-start(f32[2,32,12,512]{3,0,2,1:T(2,128)} %copy.92), calls=%async_computation.6 | async-start | bytes 3145728 | tf_op jit(solution)/shard_map/all_to_all | solution.py:91
  456.2 75.4 %all-gather.2.cloned.1.call-start = ((), (), s32[]{:S(2)}) async-start(), calls=%async_computation.7 | async-start | bytes 3538944 | tf_op jit(solution)/shard_map/all_gather | solution.py:117
  464.0 34.0 %copy-start.2 = (f32[3,384,512]{2,1,0:T(8,128)S(1)}, f32[3,384,512]{2,1,0:T(8,128)}, u32[]{:S(2)}) copy-start(f32[3,384,512]{2,1,0:T(8,128)} %copy-done.1) | copy-start | bytes 7077892
  464.0 34.0 %copy-start.6 = (f32[512]{0:T(512)S(1)}, f32[512]{0:T(512)}, u32[]{:S(2)}) copy-start(f32[512]{0:T(512)} %param.12) | copy-start | bytes 6148
Sparse Core Ops, SparseCore 0:
  500.8 30.8 all-gather.1
where the time goes:
time: 548 us; the launch traced here: 544 us
  waiting for transfers between devices  319 us (58%)
  matrix products  95.5 us (17%)
  starting transfers between devices  61.3 us (11%)
  local copies, waits for them, and re-layouts  41.5 us (8%)
  between operations  14 us (3%)
  other arithmetic  13.5 us (2%)
    all_to_all x2, waiting for transfers between devices, sequence_conv(): lax.all_to_all(sectioned[0], 'seq', split_axis=1, concat_axis=2, tiled=True)  95 us
    dot_general x16, matrix products, contract(): return jnp.einsum(pattern, first_op, second_op, precision=highest)  89.8 us
    all_to_all x2, waiting for transfers between devices, sequence_conv(): lax.all_to_all(sectioned[1], 'seq', split_axis=1, concat_axis=2, tiled=True)  88.2 us
    all_to_all x1, waiting for transfers between devices, sequence_conv(): lax.all_to_all(planes, 'seq', split_axis=2, concat_axis=1, tiled=True)  36.7 us
    all_to_all x1, waiting for transfers between devices, sequence_conv(): lax.all_to_all(sectioned[0], 'seq', split_axis=2, concat_axis=1, tiled=True)  34.6 us
    all_to_all x1, waiting for transfers between devices, sequence_conv(): lax.all_to_all(sectioned[1], 'seq', split_axis=2, concat_axis=1, tiled=True)  33.1 us
    all_gather x1, waiting for transfers between devices, on_device(): lax.all_gather(mixed, 'ch', axis=1, tiled=True)  31 us
    all_to_all x2, starting transfers between devices, sequence_conv(): lax.all_to_all(sectioned[1], 'seq', split_axis=1, concat_axis=2, tiled=True)  15.6 us
  transfers between devices with their start and end apart: 9, of which 8 were waited for; matrix products, arithmetic and copies ran while one was open for 8% of the time, Pallas kernels for 0%

commit v1 on v0

--- a/solution.py
+++ b/solution.py
@@ -5,6 +5,25 @@
 from jax.sharding import PartitionSpec as P
 
 highest = lax.Precision.HIGHEST
+
+
+def ring_gather(x, axis, dim):
+    size, mine, span = (lax.axis_size(axis), lax.axis_index(axis), x.shape[dim])
+    right = [(i, (i + 1) % size) for i in range(size)]
+    left = [(i, (i - 1) % size) for i in range(size)]
+    out = jnp.zeros((*x.shape[:dim], size * span, *x.shape[dim + 1 :]), x.dtype)
+    out = lax.dynamic_update_slice_in_dim(out, x, mine * span, axis=dim)
+    from_left = from_right = x
+    middle = size // 2
+    for step in range(1, middle + 1):
+        from_left = lax.ppermute(from_left, axis, right)
+        out = lax.dynamic_update_slice_in_dim(out, from_left, (mine - step) % size * span, axis=dim)
+        if step < size - middle:
+            from_right = lax.ppermute(from_right, axis, left)
+            out = lax.dynamic_update_slice_in_dim(
+                out, from_right, (mine + step) % size * span, axis=dim
+            )
+    return out
 
 
 def shifted(block, axis, distance):
@@ -113,11 +132,7 @@
     long_out = sequence_conv(mixed_in, long_filter)
     filtered = long_out + skip_gain * mixed_in
     mixed = (gate_late * filtered).astype(jnp.bfloat16)
-    summed = jnp.dot(
-        lax.all_gather(mixed, "ch", axis=1, tiled=True),
-        out_weight,
-        preferred_element_type=jnp.float32,
-    )
+    summed = jnp.dot(ring_gather(mixed, "ch", 1), out_weight, preferred_element_type=jnp.float32)
     return summed.astype(jnp.bfloat16)
 
 

time: 548 us -> 541 us (0.987)
  waiting for transfers between devices: 319 us -> 301 us
  between operations: 14 us -> 0.67 us
  starting transfers between devices: 61.3 us -> 74.6 us
  local copies, waits for them, and re-layouts: 41.5 us -> 50.7 us
    all_gather x1 -> x0, waiting for transfers between devices: 31 us -> none  [on_device(): lax.all_gather(mixed, 'ch', axis=1, tiled=True)]
    ppermute x0 -> x7, starting transfers between devices: none -> 13.5 us  [the longest x4 12.2 us: ring_gather(): from_left = lax.ppermute(from_left, axis, right)]
    ppermute x0 -> x7, waiting for transfers between devices: none -> 12.7 us  [the longest x4 12.7 us: ring_gather(): from_left = lax.ppermute(from_left, axis, right)]
    dynamic_update_slice x0 -> x7, local copies, waits for them, and re-layouts: none -> 5.77 us  [the longest x4 3.31 us: ring_gather(): lax.dynamic_update_slice_in_dim(out, from_left, (mine - step) % size * sp...]
  transfers between devices with their start and end apart: 9 -> 15, of which waited for: 8 -> 11; matrix products, arithmetic and copies ran while one was open for 8% -> 9% of each run, Pallas kernels for 0% -> 0%
where the time goes in v1:
time: 541 us; the launch traced here: 532 us
  waiting for transfers between devices  301 us (56%)
  matrix products  94.2 us (17%)
  starting transfers between devices  74.6 us (14%)
  local copies, waits for them, and re-layouts  50.7 us (9%)
  other arithmetic  11.2 us (2%)
    all_to_all x2, waiting for transfers between devices, sequence_conv(): lax.all_to_all(sectioned[0], 'seq', split_axis=1, concat_axis=2, tiled=True)  95 us
    dot_general x16, matrix products, contract(): return jnp.einsum(pattern, first_op, second_op, precision=highest)  89.8 us
    all_to_all x2, waiting for transfers between devices, sequence_conv(): lax.all_to_all(sectioned[1], 'seq', split_axis=1, concat_axis=2, tiled=True)  88.6 us
    all_to_all x1, waiting for transfers between devices, sequence_conv(): lax.all_to_all(planes, 'seq', split_axis=2, concat_axis=1, tiled=True)  36.6 us
    all_to_all x1, waiting for transfers between devices, sequence_conv(): lax.all_to_all(sectioned[0], 'seq', split_axis=2, concat_axis=1, tiled=True)  34.6 us
    all_to_all x1, waiting for transfers between devices, sequence_conv(): lax.all_to_all(sectioned[1], 'seq', split_axis=2, concat_axis=1, tiled=True)  33.1 us
    all_to_all x2, starting transfers between devices, sequence_conv(): lax.all_to_all(sectioned[1], 'seq', split_axis=1, concat_axis=2, tiled=True)  15.8 us
    all_to_all x2, starting transfers between devices, sequence_conv(): lax.all_to_all(sectioned[0], 'seq', split_axis=1, concat_axis=2, tiled=True)  15 us
  transfers between devices with their start and end apart: 15, of which 11 were waited for; matrix products, arithmetic and copies ran while one was open for 9% of the time, Pallas kernels for 0%

profile of v1, /device:TPU:1, one launch (start us, length us, event | category | flops | bytes accessed | tf_op | source)
XLA Modules:
  0.0 532.0 jit_solution(5726462800146568762)
XLA Ops:
  12.6 12.5 %all-to-all-start = ((f32[2,1,384,512]{3,0,1,2:T(2,128)}), f32[2,1,384,512]{3,0,1,2:T(2,128)S(1)}, u32[]{:S(2)}, u32[]{:S(2)}) async-start(f32[2,1,384,512]{3,0,1,2:T(2,128)} %copy.68), calls=%async_computation | async-start | bytes 3145728 | tf_op jit(solution)/shard_map/all_to_all | solution.py:74
  25.2 36.6 %all-to-all-done = f32[2,1,384,512]{3,0,1,2:T(2,128)S(1)} async-done(((f32[2,1,384,512]{3,0,1,2:T(2,128)}), f32[2,1,384,512]{3,0,1,2:T(2,128)S(1)}, u32[]{:S(2)}, u32[]{:S(2)}) %all-to-all-start) | async-done | bytes 1572896 | tf_op jit(solution)/shard_map/all_to_all | solution.py:74
  74.0 5.9 %fusion = (f32[4,32,12,512]{3,1,2,0:T(8,128)S(1)}, f32[4,32,12,512]{3,1,2,0:T(8,128)}) fusion(f32[4,12,512,32]{2,3,1,0:T(8,128)S(1)} %convolution_subtract_fusion, f32[32,12]{0,1:T(8,128)S(1)} %get-tuple-element.29, f32[32,12]{0,1:T(8,128)S(1)} %get-tuple-element.28, f32[4,12,512,32]{2,3,1,0:T(8,128)S(1)} %fusion.2, ...), kind=kOutput, calls=%fused_computation.4 | convolution fusion | flops 309868544 | bytes 15731712 | tf_op jit(solution)/shard_map/kp,xpbc->xkbc/dot_general | solution.py:42
  83.7 7.3 %all-to-all-start.1 = ((f32[4,32,12,512]{3,0,2,1:T(4,128)}), f32[4,32,12,512]{3,0,2,1:T(4,128)S(1)}, u32[]{:S(2)}, u32[]{:S(2)}) async-start(f32[4,32,12,512]{3,0,2,1:T(4,128)} %copy.79), calls=%async_computation.1 | async-start | bytes 6291456 | tf_op jit(solution)/shard_map/all_to_all | solution.py:93
  91.0 5.5 %copy.81 = f32[4,32,12,512]{3,0,2,1:T(4,128)} copy(f32[4,32,12,512]{3,1,2,0:T(8,128)} %get-tuple-element.10) | data formatting | bytes 6291456 | tf_op jit(solution)/shard_map/add | solution.py:57
  96.5 65.8 %all-to-all-done.1 = f32[4,32,12,512]{3,0,2,1:T(4,128)S(1)} async-done(((f32[4,32,12,512]{3,0,2,1:T(4,128)}), f32[4,32,12,512]{3,0,2,1:T(4,128)S(1)}, u32[]{:S(2)}, u32[]{:S(2)}) %all-to-all-start.1) | async-done | bytes 3145760 | tf_op jit(solution)/shard_map/all_to_all | solution.py:93
  164.0 7.8 %all-to-all-start.2 = ((f32[4,32,12,512]{3,0,2,1:T(4,128)}), f32[4,32,12,512]{3,0,2,1:T(4,128)}, u32[]{:S(2)}, u32[]{:S(2)}) async-start(f32[4,32,12,512]{3,0,2,1:T(4,128)} %copy.81), calls=%async_computation.2 | async-start | bytes 6291456 | tf_op jit(solution)/shard_map/all_to_all | solution.py:94
  175.1 9.8 %fusion.43 = f32[4,512,384]{2,1,0:T(8,128)} fusion(f32[4,384,512]{1,2,0:T(8,128)S(1)} %copy.80), kind=kOutput, calls=%fused_computation.73 | convolution fusion | flops 3625205760 | bytes 6291456 | tf_op jit(solution)/shard_map/mb,xkbc->xkmc/dot_general | solution.py:42
  184.9 60.3 %all-to-all-done.2 = f32[4,32,12,512]{3,0,2,1:T(4,128)} async-done(((f32[4,32,12,512]{3,0,2,1:T(4,128)}), f32[4,32,12,512]{3,0,2,1:T(4,128)}, u32[]{:S(2)}, u32[]{:S(2)}) %all-to-all-start.2) | async-done | bytes 3145760 | tf_op jit(solution)/shard_map/all_to_all | solution.py:94
  250.4 10.7 %fusion.41 = f32[4,512,384]{2,1,0:T(8,128)S(1)} fusion(f32[4,384,512]{1,2,0:T(8,128)} %copy.82), kind=kOutput, calls=%fused_computation.71 | convolution fusion | flops 3625205760 | bytes 6291456 | tf_op jit(solution)/shard_map/mb,xkbc->xkmc/dot_general | solution.py:42
  261.1 9.2 %subtract_bitcast_fusion = f32[4,1,384,512]{2,3,0,1:T(8,128)S(1)} fusion(f32[4,512,384]{2,1,0:T(8,128)S(1)} %copy-done.4, f32[4,384,512]{1,2,0:T(8,128)S(1)} %copy-done), kind=kOutput, calls=%fused_computation.9 | convolution fusion | flops 3625992192 | bytes 9437184 | tf_op jit(solution)/shard_map/mb,xkbc->xkmc/dot_general | solution.py:42
  270.4 9.0 %add_bitcast_fusion = f32[4,1,384,512]{2,3,0,1:T(8,128)S(1)} fusion(f32[4,512,384]{2,1,0:T(8,128)S(1)} %fusion.41, f32[4,384,512]{1,2,0:T(8,128)S(1)} %copy.80), kind=kOutput, calls=%fused_computation.8 | convolution fusion | flops 3625992192 | bytes 9437184 | tf_op jit(solution)/shard_map/mb,xkbc->xkmc/dot_general | solution.py:42
  279.7 5.4 %fusion.12 = f32[2,512,384]{2,1,0:T(8,128)S(1)} fusion(f32[2,1,384,512]{2,3,0,1:T(8,128)S(1)} %get-tuple-element.12), kind=kOutput, calls=%fused_computation.30 | convolution fusion | flops 1813266432 | bytes 3145728 | tf_op jit(solution)/shard_map/mb,xkmc->xkbc/dot_general | solution.py:42
  285.1 5.8 %fusion.10 = f32[2,512,384]{2,1,0:T(8,128)S(1)} fusion(f32[2,1,384,512]{2,3,0,1:T(8,128)S(1)} %get-tuple-element.12), kind=kOutput, calls=%fused_computation.28 | convolution fusion | flops 1813266432 | bytes 3145728 | tf_op jit(solution)/shard_map/mb,xkmc->xkbc/dot_general | solution.py:42
  290.9 5.4 %fusion.18 = f32[2,512,384]{2,1,0:T(8,128)S(1)} fusion(f32[2,512,384]{2,1,0:T(8,128)S(1)} %fusion.12, f32[2,1,384,512]{2,3,0,1:T(8,128)S(1)} %get-tuple-element.11), kind=kOutput, calls=%fused_computation.40 | convolution fusion | flops 1813659648 | bytes 4718592 | tf_op jit(solution)/shard_map/mb,xkmc->xkbc/dot_general | solution.py:42
  296.4 5.5 %fusion.7 = (f32[2,1,384,512]{2,3,0,1:T(8,128)S(1)}, f32[2,1,384,512]{2,3,0,1:T(8,128)S(1)}) fusion(f32[2,512,384]{2,1,0:T(8,128)S(1)} %fusion.18, f32[384]{0:T(512)S(1)} %get-tuple-element.34, f32[384]{0:T(512)S(1)} %get-tuple-element.35, f32[2,512,384]{2,1,0:T(8,128)S(1)} %fusion.10, f32[2,1,384,512]{2,3,0,1:T(8,128)S(1)} %get-tuple-element.11), kind=kOutput, calls=%fused_computation.23 | convolution fusion | flops 1816018944 | bytes 7867392 | tf_op jit(solution)/shard_map/mb,xkmc->xkbc/dot_general | solution.py:42
  303.9 5.7 %all-to-all-start.3 = ((f32[2,1,384,512]{3,0,1,2:T(2,128)}), f32[2,1,384,512]{3,0,1,2:T(2,128)S(1)}, u32[]{:S(2)}, u32[]{:S(2)}) async-start(f32[2,1,384,512]{3,0,1,2:T(2,128)} %copy.85), calls=%async_computation.3 | async-start | bytes 3145728 | tf_op jit(solution)/shard_map/all_to_all | solution.py:102
  311.8 34.6 %all-to-all-done.3 = f32[2,1,384,512]{3,0,1,2:T(2,128)S(1)} async-done(((f32[2,1,384,512]{3,0,1,2:T(2,128)}), f32[2,1,384,512]{3,0,1,2:T(2,128)S(1)}, u32[]{:S(2)}, u32[]{:S(2)}) %all-to-all-start.3) | async-done | bytes 1572896 | tf_op jit(solution)/shard_map/all_to_all | solution.py:102
  346.4 7.7 %all-to-all-start.4 = ((f32[2,1,384,512]{3,0,1,2:T(2,128)}), f32[2,1,384,512]{3,0,1,2:T(2,128)S(1)}, u32[]{:S(2)}, u32[]{:S(2)}) async-start(f32[2,1,384,512]{3,0,1,2:T(2,128)} %copy.87), calls=%async_computation.4 | async-start | bytes 3145728 | tf_op jit(solution)/shard_map/all_to_all | solution.py:103
  357.8 33.1 %all-to-all-done.4 = f32[2,1,384,512]{3,0,1,2:T(2,128)S(1)} async-done(((f32[2,1,384,512]{3,0,1,2:T(2,128)}), f32[2,1,384,512]{3,0,1,2:T(2,128)S(1)}, u32[]{:S(2)}, u32[]{:S(2)}) %all-to-all-start.4) | async-done | bytes 1572896 | tf_op jit(solution)/shard_map/all_to_all | solution.py:103
  397.3 7.8 %all-to-all-start.5 = ((f32[2,32,12,512]{3,0,2,1:T(2,128)}), f32[2,32,12,512]{3,0,2,1:T(2,128)}, u32[]{:S(2)}, u32[]{:S(2)}) async-start(f32[2,32,12,512]{3,0,2,1:T(2,128)} %copy.89), calls=%async_computation.5 | async-start | bytes 3145728 | tf_op jit(solution)/shard_map/all_to_all | solution.py:109
  412.7 29.2 %all-to-all-done.5 = f32[2,32,12,512]{3,0,2,1:T(2,128)} async-done(((f32[2,32,12,512]{3,0,2,1:T(2,128)}), f32[2,32,12,512]{3,0,2,1:T(2,128)}, u32[]{:S(2)}, u32[]{:S(2)}) %all-to-all-start.5) | async-done | bytes 1572896 | tf_op jit(solution)/shard_map/all_to_all | solution.py:109
  441.9 8.0 %all-to-all-start.6 = ((f32[2,32,12,512]{3,0,2,1:T(2,128)}), f32[2,32,12,512]{3,0,2,1:T(2,128)}, u32[]{:S(2)}, u32[]{:S(2)}) async-start(f32[2,32,12,512]{3,0,2,1:T(2,128)} %copy.92), calls=%async_computation.6 | async-start | bytes 3145728 | tf_op jit(solution)/shard_map/all_to_all | solution.py:110
  458.3 28.3 %all-to-all-done.6 = f32[2,32,12,512]{3,0,2,1:T(2,128)} async-done(((f32[2,32,12,512]{3,0,2,1:T(2,128)}), f32[2,32,12,512]{3,0,2,1:T(2,128)}, u32[]{:S(2)}, u32[]{:S(2)}) %all-to-all-start.6) | async-done | bytes 1572896 | tf_op jit(solution)/shard_map/all_to_all | solution.py:110
  (89 shorter events, 114.4 us)
Async XLA Ops:
  0.7 5.3 collective-permute-start
  8.3 1.8 copy-start.1
  8.3 1.7 copy-start.9
  12.6 49.3 %all-to-all-start = ((f32[2,1,384,512]{3,0,1,2:T(2,128)}), f32[2,1,384,512]{3,0,1,2:T(2,128)S(1)}, u32[]{:S(2)}, u32[]{:S(2)}) async-start(f32[2,1,384,512]{3,0,1,2:T(2,128)} %copy.68), calls=%async_computation | async-start | bytes 3145728 | tf_op jit(solution)/shard_map/all_to_all | solution.py:74
  83.7 78.6 %all-to-all-start.1 = ((f32[4,32,12,512]{3,0,2,1:T(4,128)}), f32[4,32,12,512]{3,0,2,1:T(4,128)S(1)}, u32[]{:S(2)}, u32[]{:S(2)}) async-start(f32[4,32,12,512]{3,0,2,1:T(4,128)} %copy.79), calls=%async_computation.1 | async-start | bytes 6291456 | tf_op jit(solution)/shard_map/all_to_all | solution.py:93
  162.3 1.7 copy-start.3
  164.0 81.2 %all-to-all-start.2 = ((f32[4,32,12,512]{3,0,2,1:T(4,128)}), f32[4,32,12,512]{3,0,2,1:T(4,128)}, u32[]{:S(2)}, u32[]{:S(2)}) async-start(f32[4,32,12,512]{3,0,2,1:T(4,128)} %copy.81), calls=%async_computation.2 | async-start | bytes 6291456 | tf_op jit(solution)/shard_map/all_to_all | solution.py:94
  250.4 10.7 %copy-start = (f32[4,384,512]{1,2,0:T(8,128)S(1)}, f32[4,384,512]{1,2,0:T(8,128)}, u32[]{:S(2)}) copy-start(f32[4,384,512]{1,2,0:T(8,128)} %copy.82) | copy-start | bytes 9437188
  250.4 10.7 %copy-start.4 = (f32[4,512,384]{2,1,0:T(8,128)S(1)}, f32[4,512,384]{2,1,0:T(8,128)}, u32[]{:S(2)}) copy-start(f32[4,512,384]{2,1,0:T(8,128)} %fusion.43) | copy-start | bytes 9437188
  303.9 42.4 %all-to-all-start.3 = ((f32[2,1,384,512]{3,0,1,2:T(2,128)}), f32[2,1,384,512]{3,0,1,2:T(2,128)S(1)}, u32[]{:S(2)}, u32[]{:S(2)}) async-start(f32[2,1,384,512]{3,0,1,2:T(2,128)} %copy.85), calls=%async_computation.3 | async-start | bytes 3145728 | tf_op jit(solution)/shard_map/all_to_all | solution.py:102
  346.4 44.5 %all-to-all-start.4 = ((f32[2,1,384,512]{3,0,1,2:T(2,128)}), f32[2,1,384,512]{3,0,1,2:T(2,128)S(1)}, u32[]{:S(2)}, u32[]{:S(2)}) async-start(f32[2,1,384,512]{3,0,1,2:T(2,128)} %copy.87), calls=%async_computation.4 | async-start | bytes 3145728 | tf_op jit(solution)/shard_map/all_to_all | solution.py:103
  397.3 44.6 %all-to-all-start.5 = ((f32[2,32,12,512]{3,0,2,1:T(2,128)}), f32[2,32,12,512]{3,0,2,1:T(2,128)}, u32[]{:S(2)}, u32[]{:S(2)}) async-start(f32[2,32,12,512]{3,0,2,1:T(2,128)} %copy.89), calls=%async_computation.5 | async-start | bytes 3145728 | tf_op jit(solution)/shard_map/all_to_all | solution.py:109
  441.9 44.8 %all-to-all-start.6 = ((f32[2,32,12,512]{3,0,2,1:T(2,128)}), f32[2,32,12,512]{3,0,2,1:T(2,128)}, u32[]{:S(2)}, u32[]{:S(2)}) async-start(f32[2,32,12,512]{3,0,2,1:T(2,128)} %copy.92), calls=%async_computation.6 | async-start | bytes 3145728 | tf_op jit(solution)/shard_map/all_to_all | solution.py:110
  490.6 1.9 copy-start.2
  490.7 1.9 copy-start.10
  491.6 1.8 copy-start.7
  495.4 9.5 %collective-permute-start.1 = (bf16[384,512]{1,0:T(8,128)(2,1)S(1)}, bf16[384,512]{1,0:T(8,128)(2,1)S(1)}, u32[]{:S(2)}, u32[]{:S(2)}) collective-permute-start(bf16[384,512]{1,0:T(8,128)(2,1)S(1)} %get-tuple-element.8), channel_id=1, source_target_pairs={{0,1},{1,2},{2,3},{3,4},{4,5},{5,6},{6,7},{7,0},{8,9},{9,10},{10,1... | collective-permute-start | bytes 1179656 | tf_op jit(solution)/shard_map/ppermute | solution.py:19
  500.2 7.2 %collective-permute-start.2 = (bf16[384,512]{1,0:T(8,128)(2,1)S(1)}, bf16[384,512]{1,0:T(8,128)(2,1)S(1)}, u32[]{:S(2)}, u32[]{:S(2)}) collective-permute-start(bf16[384,512]{1,0:T(8,128)(2,1)S(1)} %get-tuple-element.8), channel_id=1, source_target_pairs={{0,7},{1,0},{2,1},{3,2},{4,3},{5,4},{6,5},{7,6},{8,15},{9,8},{10,9... | collective-permute-start | bytes 1179656 | tf_op jit(solution)/shard_map/ppermute | solution.py:22
  504.9 7.2 %collective-permute-start.3 = (bf16[384,512]{1,0:T(8,128)(2,1)S(1)}, bf16[384,512]{1,0:T(8,128)(2,1)S(1)}, u32[]{:S(2)}, u32[]{:S(2)}) collective-permute-start(bf16[384,512]{1,0:T(8,128)(2,1)S(1)} %collective-permute-done.1), channel_id=1, source_target_pairs={{0,1},{1,2},{2,3},{3,4},{4,5},{5,6},{6,7},{7,0},{8,9},{9,10},{10,1... | collective-permute-start | bytes 1179656 | tf_op jit(solution)/shard_map/ppermute | solution.py:19
  507.4 8.0 %collective-permute-start.4 = (bf16[384,512]{1,0:T(8,128)(2,1)S(1)}, bf16[384,512]{1,0:T(8,128)(2,1)S(1)}, u32[]{:S(2)}, u32[]{:S(2)}) collective-permute-start(bf16[384,512]{1,0:T(8,128)(2,1)S(1)} %collective-permute-done.2), channel_id=1, source_target_pairs={{0,7},{1,0},{2,1},{3,2},{4,3},{5,4},{6,5},{7,6},{8,15},{9,8},{10,9... | collective-permute-start | bytes 1179656 | tf_op jit(solution)/shard_map/ppermute | solution.py:22
  512.1 7.2 %collective-permute-start.5 = (bf16[384,512]{1,0:T(8,128)(2,1)S(1)}, bf16[384,512]{1,0:T(8,128)(2,1)S(1)}, u32[]{:S(2)}, u32[]{:S(2)}) collective-permute-start(bf16[384,512]{1,0:T(8,128)(2,1)S(1)} %collective-permute-done.3), channel_id=1, source_target_pairs={{0,1},{1,2},{2,3},{3,4},{4,5},{5,6},{6,7},{7,0},{8,9},{9,10},{10,1... | collective-permute-start | bytes 1179656 | tf_op jit(solution)/shard_map/ppermute | solution.py:19
  515.4 12.0 %copy-start.11 = (bf16[4096,512]{1,0:T(8,128)(2,1)S(1)}, bf16[4096,512]{1,0:T(8,128)(2,1)}, u32[]{:S(2)}) copy-start(bf16[4096,512]{1,0:T(8,128)(2,1)} %param.13) | copy-start | bytes 12582916
  515.4 8.9 %collective-permute-start.6 = (bf16[384,512]{1,0:T(8,128)(2,1)S(1)}, bf16[384,512]{1,0:T(8,128)(2,1)S(1)}, u32[]{:S(2)}, u32[]{:S(2)}) collective-permute-start(bf16[384,512]{1,0:T(8,128)(2,1)S(1)} %collective-permute-done.4), channel_id=1, source_target_pairs={{0,7},{1,0},{2,1},{3,2},{4,3},{5,4},{6,5},{7,6},{8,15},{9,8},{10,9... | collective-permute-start | bytes 1179656 | tf_op jit(solution)/shard_map/ppermute | solution.py:22
  519.3 7.2 %collective-permute-start.7 = (bf16[384,512]{1,0:T(8,128)(2,1)S(1)}, bf16[384,512]{1,0:T(8,128)(2,1)S(1)}, u32[]{:S(2)}, u32[]{:S(2)}) collective-permute-start(bf16[384,512]{1,0:T(8,128)(2,1)S(1)} %collective-permute-done.5), channel_id=1, source_target_pairs={{0,1},{1,2},{2,3},{3,4},{4,5},{5,6},{6,7},{7,0},{8,9},{9,10},{10,1... | collective-permute-start | bytes 1179656 | tf_op jit(solution)/shard_map/ppermute | solution.py:19
  (3 other events, 4.5 us)
